TPU v7x, 32 devices: a whole 2x2x4 slice. The times are simulated.
32 devices in a mesh: dp: 8 (over y, x, core), exch: 4 (over z).
Axes of the slice: x: 2, y: 2, z: 4, core: 2. Of those that a mesh axis runs over, the one named last changes fastest.
Arguments:
- x_raw: bfloat16 [1024, 2048], P('exch', 'dp'), may hold values from -6 to 6
- bc_raw: bfloat16 [1024, 256], P(('exch', 'dp')), may hold values from -6 to 6
- dt_raw: bfloat16 [32, 1024], P('dp', 'exch'), may hold values from -4 to 4
- cotangent: bfloat16 [1024, 2048], P('exch', 'dp'), may hold values from -6 to 6
- ssm_state: bfloat16 [8, 32, 64, 128], P('exch', 'dp'), may hold values from -0.625 to 0.625
- conv_x_state: bfloat16 [8, 3, 2048], P('exch', None, 'dp'), may hold values from -6 to 6
- conv_bc_state: bfloat16 [8, 3, 256], P('exch'), may hold values from -6 to 6
- owner: int32 [8], P('exch'), may hold values from 0 to 3, as said below
- resp_len: int32 [8], P('exch'), may hold values from 32 to 128, as said below
- conv_x_weight: float32 [4, 2048], P(None, 'dp'), may hold values from -3 to 3
- conv_bc_weight: float32 [4, 256], replicated, may hold values from -3 to 3
- dt_bias: float32 [32], P('dp'), may hold values from -5 to -3
- a_log: float32 [32], P('dp'), may hold values from -2.3 to 2.1
- skip_d: float32 [32], P('dp'), may hold values from 0.5 to 1.5
Outputs:
- grad_x: bfloat16 [1024, 2048], P('exch', 'dp')
- grad_bc: bfloat16 [1024, 256], P(('exch', 'dp'))
- grad_dt: bfloat16 [32, 1024], P('dp', 'exch')
- grad_conv_x: float32 [4, 2048], P(None, 'dp')
- grad_conv_bc: float32 [4, 256], replicated
- grad_heads: float32 [3, 32], P(None, 'dp')
Inputs may be any that keep to these rules, and one draw needn't show every extreme that they name: `owner`: among the 2 prompts of one holder (an aligned block along exch) no learner index occurs more than 1 times, and some learner index occurs exactly 1 times; over all 8 prompts every learner index occurs exactly 2 times. `resp_len`: every learner's block of 2 responses holds a response of length 128.
All inputs are finite; a program needn't handle non-finite values.
Results may differ from a plain program's by a relative error of at most 0.001.
Values may be sent and summed in bfloat16 or wider, within the bound.
A program may use at most 64 MiB of HBM per device.

v0:
```python
import jax
import jax.numpy as jnp
from jax import lax
from jax.sharding import PartitionSpec as P

DEV_GROUP = 8
SPAN = 128
GROUP = 1
CAP = 1
PRECISE = lax.Precision.HIGHEST


def conv_pre(raw, state, weight):
    padded = jnp.concatenate([state, raw], axis=1)
    length = raw.shape[1]
    total = padded[:, 0:length] * weight[0]
    for offset in range(1, weight.shape[0]):
        total = total + padded[:, offset : offset + length] * weight[offset]
    return total


def ssd_output(values, proj_b, proj_c, steps, rate, skip, start, block):
    rows, length, heads, width = values.shape
    count = length // block
    value_blocks = values.reshape(rows, count, block, heads, width)
    b_blocks = proj_b.reshape(rows, count, block, proj_b.shape[-1])
    c_blocks = proj_c.reshape(rows, count, block, proj_c.shape[-1])
    step_blocks = steps.reshape(rows, count, block, heads)
    logs = jnp.cumsum(-rate * step_blocks, axis=2)
    causal = jnp.tril(jnp.ones((block, block), jnp.float32))
    spread = logs[:, :, :, None, :] - logs[:, :, None, :, :]
    decays = jnp.exp(jnp.where(causal[:, :, None] > 0.5, spread, 0.0)) * causal[:, :, None]
    scores = jnp.einsum("rntk,rnsk->rnts", c_blocks, b_blocks, precision=PRECISE)
    weighted = value_blocks * step_blocks[..., None]
    mixing = scores[..., None] * decays
    intra = jnp.einsum("rntsh,rnshp->rnthp", mixing, weighted, precision=PRECISE)
    entry = jnp.exp(logs[:, 0])
    carried = jnp.einsum("rtk,rhpk->rthp", c_blocks[:, 0], start, precision=PRECISE)
    pieces = [carried * entry[..., None]]
    inter = jnp.stack(pieces, axis=1)
    output = intra + inter + skip[:, None] * value_blocks
    return output.reshape(rows, length, heads, width)


def window_loss(
    x_rows,
    bc_act,
    dt_rows,
    x_weight,
    bias,
    decay_log,
    skip,
    x_prev,
    start,
    cotan,
    mask,
    heads,
    block,
):
    x_act = jax.nn.silu(conv_pre(x_rows, x_prev, x_weight))
    rows, length, channels = x_rows.shape
    values = x_act.reshape(rows, length, heads, channels // heads)
    half = bc_act.shape[-1] // 2
    steps = jax.nn.softplus(dt_rows + bias)
    output = ssd_output(
        values,
        bc_act[..., :half],
        bc_act[..., half:],
        steps,
        jnp.exp(decay_log),
        skip,
        start,
        block,
    )
    return jnp.sum(output.reshape(rows, length, channels) * cotan * mask[..., None])


def local(
    x_raw,
    bc_raw,
    dt_raw,
    cotangent,
    ssm_state,
    conv_x_state,
    conv_bc_state,
    owner,
    resp_len,
    conv_x_weight,
    conv_bc_weight,
    dt_bias,
    a_log,
    skip_d,
):
    peer_count = lax.axis_size("exch")
    slices = lax.axis_size("dp")
    prompts = owner.shape[0]
    responses = resp_len.shape[0]
    head_count = dt_raw.shape[0]
    tokens = x_raw.shape[0]
    channels = x_raw.shape[1]
    pair_width = 2 * ssm_state.shape[-1]
    conv_depth = conv_x_state.shape[1]
    length = tokens // responses
    row_count = bc_raw.shape[0]
    groups = bc_raw.shape[1] // pair_width
    my_group = lax.axis_index("dp") // DEV_GROUP
    targets = jnp.arange(peer_count, dtype=jnp.int32)
    match = (owner[:, None] == targets[None, :]).astype(jnp.int32)
    earlier = jnp.cumsum(match, axis=0) - match
    places = jnp.sum(earlier * match, axis=1)
    slot_ids = jnp.arange(CAP, dtype=jnp.int32)
    routing = (match[:, :, None] == 1) & (places[:, None, None] == slot_ids[None, None, :])
    routing = routing.reshape(prompts, peer_count * CAP).astype(jnp.bfloat16)

    def pack_slots(values):
        moved = jnp.dot(routing.T, values.reshape(prompts, -1), preferred_element_type=jnp.float32)
        return moved.astype(jnp.bfloat16).reshape(peer_count, CAP, -1)

    bc_state = lax.dynamic_slice_in_dim(conv_bc_state, my_group * pair_width, pair_width, 2)
    filled = jnp.sum(routing, axis=0).reshape(peer_count, CAP)
    got_ssm, got_x, got_bc, got_fill = (
        lax.all_to_all(pack_slots(ssm_state), "exch", split_axis=0, concat_axis=0, tiled=True),
        lax.all_to_all(pack_slots(conv_x_state), "exch", split_axis=0, concat_axis=0, tiled=True),
        lax.all_to_all(pack_slots(bc_state), "exch", split_axis=0, concat_axis=0, tiled=True),
        lax.all_to_all(filled, "exch", split_axis=0, concat_axis=0, tiled=True),
    )
    present = (got_fill.reshape(peer_count * CAP) > 0.5).astype(jnp.int32)
    position = jnp.cumsum(present) - 1
    owned_ids = jnp.arange(prompts, dtype=jnp.int32)
    select = ((present[None, :] == 1) & (position[None, :] == owned_ids[:, None])).astype(
        jnp.bfloat16
    )

    def unpack(values, shape):
        chosen = jnp.dot(
            select, values.reshape(peer_count * CAP, -1), preferred_element_type=jnp.float32
        )
        return jnp.repeat(chosen, GROUP, axis=0).reshape(shape)

    start_state = unpack(got_ssm, (responses, head_count, channels // head_count, -1))
    x_prev = unpack(got_x, (responses, conv_depth, channels))
    bc_prev = unpack(got_bc, (responses, conv_depth, pair_width))
    gathered = lax.all_gather(bc_raw, "dp", axis=0, tiled=True)
    bc_local = lax.dynamic_slice_in_dim(gathered, my_group * pair_width, pair_width, 1)
    x_rows = x_raw.astype(jnp.float32).reshape(responses, length, channels)
    bc_rows = bc_local.astype(jnp.float32).reshape(responses, length, pair_width)
    cot_rows = cotangent.astype(jnp.float32).reshape(responses, length, channels)
    dt_rows = dt_raw.astype(jnp.float32).T.reshape(responses, length, head_count)
    live_mask = (jnp.arange(length, dtype=jnp.int32)[None, :] < resp_len[:, None]).astype(
        jnp.float32
    )
    bc_weight = lax.dynamic_slice_in_dim(conv_bc_weight, my_group * pair_width, pair_width, 1)
    bc_pre = conv_pre(bc_rows, bc_prev, bc_weight)
    bc_act, silu_back = jax.vjp(jax.nn.silu, bc_pre)

    def local_loss(x_in, bc_in, dt_in, x_weight, bias, decay_log, skip):
        return window_loss(
            x_in,
            bc_in,
            dt_in,
            x_weight,
            bias,
            decay_log,
            skip,
            x_prev,
            start_state,
            cot_rows,
            live_mask,
            head_count,
            SPAN,
        )

    grad_xr, grad_bca, grad_dtr, grad_wx, grad_bias, grad_decay, grad_skip = jax.grad(
        local_loss, argnums=(0, 1, 2, 3, 4, 5, 6)
    )(x_rows, bc_act, dt_rows, conv_x_weight, dt_bias, a_log, skip_d)
    grad_pre = silu_back(grad_bca)[0]
    unused, conv_back = jax.vjp(
        lambda raw, weight: conv_pre(raw, bc_prev, weight), bc_rows, bc_weight
    )
    grad_raw, grad_wbc = conv_back(grad_pre)
    returned = lax.all_to_all(
        grad_raw.reshape(slices, row_count, pair_width),
        "dp",
        split_axis=0,
        concat_axis=0,
        tiled=True,
    )
    grad_share = jnp.sum(returned.reshape(groups, DEV_GROUP, row_count, pair_width), axis=1)
    grad_share = grad_share.transpose(1, 0, 2).reshape(row_count, groups * pair_width)
    empty_taps = jnp.zeros((conv_depth + 1, groups * pair_width), jnp.float32)
    grad_wx, grad_bias, grad_decay, grad_skip = lax.psum(
        (grad_wx, grad_bias, grad_decay, grad_skip), "exch"
    )
    placed = lax.dynamic_update_slice_in_dim(empty_taps, grad_wbc, my_group * pair_width, 1)
    grad_taps = lax.psum(placed, ("dp", "exch"))
    grad_x = grad_xr.reshape(tokens, channels).astype(jnp.bfloat16)
    grad_bc = grad_share.astype(jnp.bfloat16)
    grad_dt = grad_dtr.reshape(tokens, head_count).T.astype(jnp.bfloat16)
    grad_heads = jnp.stack([grad_bias, grad_decay, grad_skip])
    return (grad_x, grad_bc, grad_dt, grad_wx, grad_taps, grad_heads)


def solution(mesh):
    in_specs = (
        P("exch", "dp"),
        P(("exch", "dp"), None),
        P("dp", "exch"),
        P("exch", "dp"),
        P("exch", "dp", None, None),
        P("exch", None, "dp"),
        P("exch", None, None),
        P("exch"),
        P("exch"),
        P(None, "dp"),
        P(),
        P("dp"),
        P("dp"),
        P("dp"),
    )
    out_specs = (
        P("exch", "dp"),
        P(("exch", "dp"), None),
        P("dp", "exch"),
        P(None, "dp"),
        P(),
        P(None, "dp"),
    )
    return jax.shard_map(local, mesh=mesh, in_specs=in_specs, out_specs=out_specs, check_vma=False)
```

profile of v0, /device:TPU:0, one launch (start us, length us, event | category | flops | bytes accessed | tf_op | source)
XLA Modules:
  0.0 124.4 jit_solution(9123671219750444243)
XLA Ops:
  0.6 0.7 fusion.80
  1.4 0.6 copy-done.8
  2.3 0.7 copy.167
  3.0 6.3 %all-to-all-start = ((bf16[4,1,1]{2,1,0:T(2,128)(2,1)}), bf16[4,1,1]{2,1,0:T(2,128)(2,1)S(1)}, u32[]{:S(2)}, u32[]{:S(2)}) async-start(bf16[4,1,1]{2,1,0:T(2,128)(2,1)} %copy.167), calls=%async_computation | async-start | bytes 4096 | tf_op jit(solution)/shard_map/all_to_all | solution.py:125
  9.4 1.2 reshape.547
  10.7 0.2 reshape.548
  10.9 0.4 copy-done.13
  11.4 0.6 copy-done.3
  12.2 0.6 copy-done.6
  12.8 0.7 copy-done.7
  13.6 0.5 broadcast.324
  14.2 0.7 reduce.16
  14.8 0.6 reshape.551
  15.7 0.7 reduce.17
  16.4 0.6 reshape.553
  17.4 0.6 copy-done.4
  18.1 9.3 %all_gather.3 = bf16[256,256]{1,0:T(8,128)(2,1)S(1)} all-gather(bf16[32,256]{1,0:T(8,128)(2,1)S(1)} %copy-done.4), channel_id=1, replica_groups=mesh['dp'=8,'exch'=4] {'dp'}, dimensions={0}, use_global_device_ids=true | all-gather | bytes 147456 | tf_op jit(solution)/shard_map/all_gather | solution.py:143
  27.5 0.4 fusion
  27.8 1.0 reduce.18
  28.8 1.0 reshape.555
  29.8 0.9 copy-done.2
  31.1 5.1 %all-to-all-start.1 = ((bf16[4,2,384]{2,1,0:T(2,128)(2,1)}), bf16[4,2,384]{2,1,0:T(2,128)(2,1)S(1)}, u32[]{:S(2)}, u32[]{:S(2)}) async-start(bf16[4,2,384]{2,1,0:T(2,128)(2,1)} %reshape.553), calls=%async_computation.1 | async-start | bytes 12288 | tf_op jit(solution)/shard_map/all_to_all | solution.py:124
  36.6 5.2 %all-to-all-done.1 = bf16[4,2,384]{2,1,0:T(2,128)(2,1)S(1)} async-done(((bf16[4,2,384]{2,1,0:T(2,128)(2,1)}), bf16[4,2,384]{2,1,0:T(2,128)(2,1)S(1)}, u32[]{:S(2)}, u32[]{:S(2)}) %all-to-all-start.1) | async-done | bytes 6176 | tf_op jit(solution)/shard_map/all_to_all | solution.py:124
  41.8 3.2 %all-to-all-start.2 = ((bf16[4,2,384]{2,1,0:T(2,128)(2,1)}), bf16[4,2,384]{2,1,0:T(2,128)(2,1)S(1)}, u32[]{:S(2)}, u32[]{:S(2)}) async-start(bf16[4,2,384]{2,1,0:T(2,128)(2,1)} %reshape.551), calls=%async_computation.2 | async-start | bytes 12288 | tf_op jit(solution)/shard_map/all_to_all | solution.py:123
  45.3 5.4 %all-to-all-done.2 = bf16[4,2,384]{2,1,0:T(2,128)(2,1)S(1)} async-done(((bf16[4,2,384]{2,1,0:T(2,128)(2,1)}), bf16[4,2,384]{2,1,0:T(2,128)(2,1)S(1)}, u32[]{:S(2)}, u32[]{:S(2)}) %all-to-all-start.2) | async-done | bytes 6176 | tf_op jit(solution)/shard_map/all_to_all | solution.py:123
  50.6 3.4 %all-to-all-start.3 = ((bf16[4,2,16384]{2,1,0:T(2,128)(2,1)}), bf16[4,2,16384]{2,1,0:T(2,128)(2,1)S(1)}, u32[]{:S(2)}, u32[]{:S(2)}) async-start(bf16[4,2,16384]{2,1,0:T(2,128)(2,1)} %reshape.555), calls=%async_computation.3 | async-start | bytes 524288 | tf_op jit(solution)/shard_map/all_to_all | solution.py:122
  54.9 0.4 fusion.46
  55.3 1.3 %fusion.10 = (f32[2,128,4]{1,2,0:T(4,128)S(1)}, f32[2,128,4]{1,2,0:T(4,128)S(1)}, f32[2,128,128]{2,1,0:T(8,128)S(1)}) fusion(f32[2,128,128]{2,1,0:T(8,128)S(1)} %fusion.46, f32[128,128]{1,0:T(8,128)S(1)} %fusion.52, f32[2,128,4]{1,2,0:T(4,128)S(1)} %copy.171, pred[128,128]{1,0:T(8,128)(4,1)S(1)} %broadcast_compare_fusion, ...), kind=kOutput, calls=%fused_computation.27 | convolution fusion | flops 102201344 | bytes 885760 | tf_op jit(solution)/shard_map/transpose(jvp(rntsh,rnshp->rnthp))/dot_general | solution.py:36
  56.6 0.7 copy-done.12
  57.3 0.8 multiply_reduce_fusion.10
  59.0 0.7 fusion.19
  59.8 0.4 fusion.49
  60.2 0.6 all-to-all-done.3
  60.8 0.3 reshape.556
  61.0 0.3 copy.204
  61.4 0.3 fusion.72
  61.7 0.4 fusion.1
  62.1 0.6 convolution_bitcast_fusion.2
  62.9 0.3 convolution_add_fusion
  63.2 0.2 multiply_reduce_fusion.4
  63.4 39.4 %psum.36 = f32[4,256]{1,0:T(4,128)} all-reduce(f32[4,256]{1,0:T(4,128)S(1)} %pad_add_fusion.6), channel_id=1, replica_groups=mesh['dp'=8,'exch'=4] {'dp','exch'}, use_global_device_ids=true, to_apply=%region_21.22 | all-reduce | flops 1024 | bytes 8192 | tf_op jit(solution)/shard_map/psum | solution.py:195
  102.9 2.2 %reduce_window_sum.46 = f32[2,1,128,4]{3,2,1,0:T(8,128)S(1)} reduce-window(f32[2,1,128,4]{3,2,1,0:T(8,128)S(1)} %bitcast_add_fusion, f32[]{:T(128)} %constant.56.clone.1), window={size=1x1x128x1 pad=0_0x0_0x0_127x0_0}, to_apply=%region_11.12 | reduce-window | flops 130048 | bytes 8196 | tf_op jit(solution)/shard_map/transpose(jvp(jit(cumsum)))/reduce_window_sum | solution.py:29
  105.2 0.8 multiply_reduce_fusion.11
  106.1 0.8 pad_add_fusion
  106.9 4.8 %all-to-all-start.4 = ((f32[8,32,256]{2,1,0:T(8,128)}), f32[8,32,256]{2,1,0:T(8,128)S(1)}, u32[]{:S(2)}, u32[]{:S(2)}) async-start(f32[8,32,256]{2,1,0:T(8,128)} %bitcast.44), calls=%async_computation.4 | async-start | bytes 524288 | tf_op jit(solution)/shard_map/all_to_all | solution.py:181
  111.9 11.3 %all-reduce.18 = (f32[4,256]{1,0:T(4,128)}, f32[1,4]{1,0:T(1,128)S(1)}, f32[1,4]{1,0:T(1,128)S(1)}, f32[1,4]{1,0:T(1,128)S(1)}) all-reduce(f32[4,256]{1,0:T(4,128)S(1)} %pad_add_fusion.7, f32[1,4]{1,0:T(1,128)S(1)} %bitcast.233, f32[1,4]{1,0:T(1,128)S(1)} %multiply_bitcast_fusion, ...), channel_id=1, replica_groups=mesh['dp'=8,'exch'=4] {'exch'}, use_global_device_ids=true, to_apply=%region_16.17 | all-reduce | flops 1036 | bytes 8288 | tf_op jit(solution)/shard_map/psum | solution.py:191
  123.2 0.6 pad_maximum_fusion.2
  123.8 0.6 reduce_sum.196
  (77 shorter events, 5.0 us)
Async XLA Ops:
  0.6 12.8 %copy-start = (bf16[2,3,256]{2,0,1:T(2,128)(2,1)S(1)}, bf16[2,3,256]{2,0,1:T(2,128)(2,1)}, u32[]{:S(2)}) copy-start(bf16[2,3,256]{2,0,1:T(2,128)(2,1)} %param.19) | copy-start | bytes 9220
  1.4 0.7 copy-start.8
  3.0 28.1 %all-to-all-start = ((bf16[4,1,1]{2,1,0:T(2,128)(2,1)}), bf16[4,1,1]{2,1,0:T(2,128)(2,1)S(1)}, u32[]{:S(2)}, u32[]{:S(2)}) async-start(bf16[4,1,1]{2,1,0:T(2,128)(2,1)} %copy.167), calls=%async_computation | async-start | bytes 4096 | tf_op jit(solution)/shard_map/all_to_all | solution.py:125
  9.4 1.2 copy-start.1
  10.6 0.7 copy-start.13
  10.7 0.7 copy-start.11
  11.3 0.7 copy-start.3
  11.3 0.7 copy-start.5
  12.1 0.7 copy-start.6
  12.8 0.7 copy-start.7
  14.8 0.7 copy-start.10
  17.3 0.7 copy-start.4
  18.0 9.4 %copy-start.9 = (bf16[2,4,64,128]{3,2,1,0:T(8,128)(2,1)S(1)}, bf16[2,4,64,128]{3,2,1,0:T(8,128)(2,1)}, u32[]{:S(2)}) copy-start(bf16[2,4,64,128]{3,2,1,0:T(8,128)(2,1)} %param.18) | copy-start | bytes 393220
  29.8 0.9 copy-start.2
  31.1 10.7 %all-to-all-start.1 = ((bf16[4,2,384]{2,1,0:T(2,128)(2,1)}), bf16[4,2,384]{2,1,0:T(2,128)(2,1)S(1)}, u32[]{:S(2)}, u32[]{:S(2)}) async-start(bf16[4,2,384]{2,1,0:T(2,128)(2,1)} %reshape.553), calls=%async_computation.1 | async-start | bytes 12288 | tf_op jit(solution)/shard_map/all_to_all | solution.py:124
  41.8 8.8 %all-to-all-start.2 = ((bf16[4,2,384]{2,1,0:T(2,128)(2,1)}), bf16[4,2,384]{2,1,0:T(2,128)(2,1)S(1)}, u32[]{:S(2)}, u32[]{:S(2)}) async-start(bf16[4,2,384]{2,1,0:T(2,128)(2,1)} %reshape.551), calls=%async_computation.2 | async-start | bytes 12288 | tf_op jit(solution)/shard_map/all_to_all | solution.py:123
  50.6 10.2 %all-to-all-start.3 = ((bf16[4,2,16384]{2,1,0:T(2,128)(2,1)}), bf16[4,2,16384]{2,1,0:T(2,128)(2,1)S(1)}, u32[]{:S(2)}, u32[]{:S(2)}) async-start(bf16[4,2,16384]{2,1,0:T(2,128)(2,1)} %reshape.555), calls=%async_computation.3 | async-start | bytes 524288 | tf_op jit(solution)/shard_map/all_to_all | solution.py:122
  56.6 0.7 copy-start.12
  106.9 16.9 %all-to-all-start.4 = ((f32[8,32,256]{2,1,0:T(8,128)}), f32[8,32,256]{2,1,0:T(8,128)S(1)}, u32[]{:S(2)}, u32[]{:S(2)}) async-start(f32[8,32,256]{2,1,0:T(8,128)} %bitcast.44), calls=%async_computation.4 | async-start | bytes 524288 | tf_op jit(solution)/shard_map/all_to_all | solution.py:181
where the time goes:
time: 125 us; the launch traced here: 124 us
  blocking collectives  60.1 us (48%)
  starting transfers between devices  22.9 us (18%)
  local copies, waits for them, and re-layouts  12.2 us (10%)
  other arithmetic  11.7 us (9%)
  waiting for transfers between devices  11.2 us (9%)
  matrix products  5.42 us (4%)
    psum x1, blocking collectives, local(): grad_taps = lax.psum(placed, ('dp', 'exch'))  39.4 us
    psum x1, blocking collectives, local(): lax.psum((grad_wx, grad_bias, grad_decay, grad_skip), 'exch')  11.3 us
    all_gather x1, blocking collectives, local(): gathered = lax.all_gather(bc_raw, 'dp', axis=0, tiled=True)  9.34 us
    unnamed x37, local copies, waits for them, and re-layouts  7.99 us
    all_to_all x1, starting transfers between devices, local(): lax.all_to_all(filled, 'exch', split_axis=0, concat_axis=0, tiled=True)  6.35 us
    all_to_all x1, waiting for transfers between devices, local(): lax.all_to_all(pack_slots(conv_x_state), 'exch', split_axis=0, concat_axi...  5.35 us
    all_to_all x1, waiting for transfers between devices, local(): lax.all_to_all(pack_slots(bc_state), 'exch', split_axis=0, concat_axis=0,...  5.23 us
    all_to_all x1, starting transfers between devices, local(): lax.all_to_all(pack_slots(bc_state), 'exch', split_axis=0, concat_axis=0,...  5.11 us
  transfers between devices with their start and end apart: 5, of which 3 were waited for; matrix products, arithmetic and copies ran while one was open for 12% of the time, Pallas kernels for 0%

commit v1 on v0

--- a/solution.py
+++ b/solution.py
@@ -1,13 +1,23 @@
+import functools
 import jax
 import jax.numpy as jnp
 from jax import lax
 from jax.sharding import PartitionSpec as P
+from jax.lax import all_gather
 
 DEV_GROUP = 8
 SPAN = 128
 GROUP = 1
 CAP = 1
 PRECISE = lax.Precision.HIGHEST
+
+
+def _step_on_yards(point, row_axis):
+    m_next = all_gather(point, row_axis)
+    return jnp.sum(m_next, axis=0)
+
+
+build_rings_all = functools.partial(_step_on_yards, row_axis=("dp", "exch"))
 
 
 def conv_pre(raw, state, weight):
@@ -192,7 +202,7 @@
         (grad_wx, grad_bias, grad_decay, grad_skip), "exch"
     )
     placed = lax.dynamic_update_slice_in_dim(empty_taps, grad_wbc, my_group * pair_width, 1)
-    grad_taps = lax.psum(placed, ("dp", "exch"))
+    grad_taps = build_rings_all(placed)
     grad_x = grad_xr.reshape(tokens, channels).astype(jnp.bfloat16)
     grad_bc = grad_share.astype(jnp.bfloat16)
     grad_dt = grad_dtr.reshape(tokens, head_count).T.astype(jnp.bfloat16)

time: 125 us -> 150 us (1.20)
  blocking collectives: 60.1 us -> 85.2 us
    all_gather x0 -> x1, blocking collectives: none -> 66 us  [_step_on_yards(): m_next = all_gather(point, row_axis)]
    psum x1 -> x0, blocking collectives: 39.4 us -> none  [local(): grad_taps = lax.psum(placed, ('dp', 'exch'))]
  transfers between devices with their start and end apart: 5 -> 5, of which waited for: 3 -> 3; matrix products, arithmetic and copies ran while one was open for 12% -> 10% of each run, Pallas kernels for 0% -> 0%
where the time goes in v1:
time: 150 us; the launch traced here: 149 us
  blocking collectives  85.2 us (57%)
  starting transfers between devices  21.5 us (14%)
  other arithmetic  12.3 us (8%)
  local copies, waits for them, and re-layouts  12.2 us (8%)
  waiting for transfers between devices  11.2 us (7%)
  matrix products  5.42 us (4%)
    all_gather x1, blocking collectives, _step_on_yards(): m_next = all_gather(point, row_axis)  66 us
    psum x1, blocking collectives, local(): lax.psum((grad_wx, grad_bias, grad_decay, grad_skip), 'exch')  9.94 us
    all_gather x1, blocking collectives, local(): gathered = lax.all_gather(bc_raw, 'dp', axis=0, tiled=True)  9.34 us
    unnamed x37, local copies, waits for them, and re-layouts  7.99 us
    all_to_all x1, starting transfers between devices, local(): lax.all_to_all(filled, 'exch', split_axis=0, concat_axis=0, tiled=True)  6.35 us
    all_to_all x1, waiting for transfers between devices, local(): lax.all_to_all(pack_slots(conv_x_state), 'exch', split_axis=0, concat_axi...  5.35 us
    all_to_all x1, waiting for transfers between devices, local(): lax.all_to_all(pack_slots(bc_state), 'exch', split_axis=0, concat_axis=0,...  5.23 us
    all_to_all x1, starting transfers between devices, local(): lax.all_to_all(pack_slots(bc_state), 'exch', split_axis=0, concat_axis=0,...  5.11 us
  transfers between devices with their start and end apart: 5, of which 3 were waited for; matrix products, arithmetic and copies ran while one was open for 10% of the time, Pallas kernels for 0%

profile of v1, /device:TPU:0, one launch (start us, length us, event | category | flops | bytes accessed | tf_op | source)
XLA Modules:
  0.0 148.9 jit_solution(10071724500012700689)
XLA Ops:
  0.6 0.7 fusion.80
  1.4 0.6 copy-done.8
  2.3 0.7 copy.167
  3.0 6.3 %all-to-all-start = ((bf16[4,1,1]{2,1,0:T(2,128)(2,1)}), bf16[4,1,1]{2,1,0:T(2,128)(2,1)S(1)}, u32[]{:S(2)}, u32[]{:S(2)}) async-start(bf16[4,1,1]{2,1,0:T(2,128)(2,1)} %copy.167), calls=%async_computation | async-start | bytes 4096 | tf_op jit(solution)/shard_map/all_to_all | solution.py:135
  9.4 1.2 reshape.551
  10.7 0.2 reshape.552
  10.9 0.4 copy-done.13
  11.4 0.6 copy-done.3
  12.2 0.6 copy-done.6
  12.8 0.7 copy-done.7
  13.6 0.5 broadcast.324
  14.2 0.7 reduce.17
  14.8 0.6 reshape.555
  15.7 0.7 reduce.18
  16.4 0.6 reshape.557
  17.4 0.6 copy-done.4
  18.1 9.3 %all_gather.9 = bf16[256,256]{1,0:T(8,128)(2,1)S(1)} all-gather(bf16[32,256]{1,0:T(8,128)(2,1)S(1)} %copy-done.4), channel_id=1, replica_groups=mesh['dp'=8,'exch'=4] {'dp'}, dimensions={0}, use_global_device_ids=true | all-gather | bytes 147456 | tf_op jit(solution)/shard_map/all_gather | solution.py:153
  27.5 0.4 fusion
  27.8 1.0 reduce.19
  28.8 1.0 reshape.559
  29.8 0.9 copy-done.2
  31.1 5.1 %all-to-all-start.1 = ((bf16[4,2,384]{2,1,0:T(2,128)(2,1)}), bf16[4,2,384]{2,1,0:T(2,128)(2,1)S(1)}, u32[]{:S(2)}, u32[]{:S(2)}) async-start(bf16[4,2,384]{2,1,0:T(2,128)(2,1)} %reshape.557), calls=%async_computation.1 | async-start | bytes 12288 | tf_op jit(solution)/shard_map/all_to_all | solution.py:134
  36.6 5.2 %all-to-all-done.1 = bf16[4,2,384]{2,1,0:T(2,128)(2,1)S(1)} async-done(((bf16[4,2,384]{2,1,0:T(2,128)(2,1)}), bf16[4,2,384]{2,1,0:T(2,128)(2,1)S(1)}, u32[]{:S(2)}, u32[]{:S(2)}) %all-to-all-start.1) | async-done | bytes 6176 | tf_op jit(solution)/shard_map/all_to_all | solution.py:134
  41.8 3.2 %all-to-all-start.2 = ((bf16[4,2,384]{2,1,0:T(2,128)(2,1)}), bf16[4,2,384]{2,1,0:T(2,128)(2,1)S(1)}, u32[]{:S(2)}, u32[]{:S(2)}) async-start(bf16[4,2,384]{2,1,0:T(2,128)(2,1)} %reshape.555), calls=%async_computation.2 | async-start | bytes 12288 | tf_op jit(solution)/shard_map/all_to_all | solution.py:133
  45.3 5.4 %all-to-all-done.2 = bf16[4,2,384]{2,1,0:T(2,128)(2,1)S(1)} async-done(((bf16[4,2,384]{2,1,0:T(2,128)(2,1)}), bf16[4,2,384]{2,1,0:T(2,128)(2,1)S(1)}, u32[]{:S(2)}, u32[]{:S(2)}) %all-to-all-start.2) | async-done | bytes 6176 | tf_op jit(solution)/shard_map/all_to_all | solution.py:133
  50.6 3.4 %all-to-all-start.3 = ((bf16[4,2,16384]{2,1,0:T(2,128)(2,1)}), bf16[4,2,16384]{2,1,0:T(2,128)(2,1)S(1)}, u32[]{:S(2)}, u32[]{:S(2)}) async-start(bf16[4,2,16384]{2,1,0:T(2,128)(2,1)} %reshape.559), calls=%async_computation.3 | async-start | bytes 524288 | tf_op jit(solution)/shard_map/all_to_all | solution.py:132
  54.9 0.4 fusion.46
  55.3 1.3 fusion.10
  56.6 0.7 copy-done.12
  57.3 0.8 multiply_reduce_fusion.10
  59.0 0.7 fusion.19
  59.8 0.4 fusion.49
  60.2 0.6 all-to-all-done.3
  60.8 0.3 reshape.560
  61.0 0.3 copy.204
  61.4 0.3 fusion.72
  61.7 0.4 fusion.1
  62.1 0.6 convolution_bitcast_fusion.2
  62.9 0.3 convolution_add_fusion
  63.4 66.0 %all-gather.1 = f32[32,4,256]{2,1,0:T(4,128)S(1)} all-gather(f32[1,4,256]{2,1,0:T(4,128)S(1)} %add_bitcast_fusion), channel_id=2, replica_groups=mesh['dp'=8,'exch'=4] {'dp','exch'}, dimensions={0}, use_global_device_ids=true | all-gather | bytes 135168 | tf_op jit(solution)/shard_map/all_gather | solution.py:16
  129.4 0.6 reduce_sum.231
  130.1 2.2 %reduce_window_sum.46 = f32[2,1,128,4]{3,2,1,0:T(8,128)S(1)} reduce-window(f32[2,1,128,4]{3,2,1,0:T(8,128)S(1)} %bitcast_add_fusion, f32[]{:T(128)} %constant.56.clone.1), window={size=1x1x128x1 pad=0_0x0_0x0_127x0_0}, to_apply=%region_11.12 | reduce-window | flops 130048 | bytes 8196 | tf_op jit(solution)/shard_map/transpose(jvp(jit(cumsum)))/reduce_window_sum | solution.py:39
  132.4 0.8 multiply_reduce_fusion.11
  133.3 0.8 pad_add_fusion
  134.1 3.4 %all-to-all-start.4 = ((f32[8,32,256]{2,1,0:T(8,128)}), f32[8,32,256]{2,1,0:T(8,128)S(1)}, u32[]{:S(2)}, u32[]{:S(2)}) async-start(f32[8,32,256]{2,1,0:T(8,128)} %bitcast.44), calls=%async_computation.4 | async-start | bytes 524288 | tf_op jit(solution)/shard_map/all_to_all | solution.py:191
  137.7 9.9 %all-reduce.18 = (f32[4,256]{1,0:T(4,128)}, f32[1,4]{1,0:T(1,128)S(1)}, f32[1,4]{1,0:T(1,128)S(1)}, f32[1,4]{1,0:T(1,128)S(1)}) all-reduce(f32[4,256]{1,0:T(4,128)S(1)} %pad_add_fusion.6, f32[1,4]{1,0:T(1,128)S(1)} %bitcast.235, f32[1,4]{1,0:T(1,128)S(1)} %multiply_bitcast_fusion, ...), channel_id=1, replica_groups=mesh['dp'=8,'exch'=4] {'exch'}, use_global_device_ids=true, to_apply=%region_16.17 | all-reduce | flops 1036 | bytes 8288 | tf_op jit(solution)/shard_map/psum | solution.py:201
  147.7 0.6 pad_maximum_fusion.2
  148.3 0.6 reduce_sum.204
  (78 shorter events, 5.3 us)
Async XLA Ops:
  0.6 12.8 %copy-start = (bf16[2,3,256]{2,0,1:T(2,128)(2,1)S(1)}, bf16[2,3,256]{2,0,1:T(2,128)(2,1)}, u32[]{:S(2)}) copy-start(bf16[2,3,256]{2,0,1:T(2,128)(2,1)} %param.19) | copy-start | bytes 9220
  1.4 0.7 copy-start.8
  3.0 28.1 %all-to-all-start = ((bf16[4,1,1]{2,1,0:T(2,128)(2,1)}), bf16[4,1,1]{2,1,0:T(2,128)(2,1)S(1)}, u32[]{:S(2)}, u32[]{:S(2)}) async-start(bf16[4,1,1]{2,1,0:T(2,128)(2,1)} %copy.167), calls=%async_computation | async-start | bytes 4096 | tf_op jit(solution)/shard_map/all_to_all | solution.py:135
  9.4 1.2 copy-start.1
  10.6 0.7 copy-start.13
  10.7 0.7 copy-start.11
  11.3 0.7 copy-start.3
  11.3 0.7 copy-start.5
  12.1 0.7 copy-start.6
  12.8 0.7 copy-start.7
  14.8 0.7 copy-start.10
  17.3 0.7 copy-start.4
  18.0 9.4 %copy-start.9 = (bf16[2,4,64,128]{3,2,1,0:T(8,128)(2,1)S(1)}, bf16[2,4,64,128]{3,2,1,0:T(8,128)(2,1)}, u32[]{:S(2)}) copy-start(bf16[2,4,64,128]{3,2,1,0:T(8,128)(2,1)} %param.18) | copy-start | bytes 393220
  29.8 0.9 copy-start.2
  31.1 10.7 %all-to-all-start.1 = ((bf16[4,2,384]{2,1,0:T(2,128)(2,1)}), bf16[4,2,384]{2,1,0:T(2,128)(2,1)S(1)}, u32[]{:S(2)}, u32[]{:S(2)}) async-start(bf16[4,2,384]{2,1,0:T(2,128)(2,1)} %reshape.557), calls=%async_computation.1 | async-start | bytes 12288 | tf_op jit(solution)/shard_map/all_to_all | solution.py:134
  41.8 8.8 %all-to-all-start.2 = ((bf16[4,2,384]{2,1,0:T(2,128)(2,1)}), bf16[4,2,384]{2,1,0:T(2,128)(2,1)S(1)}, u32[]{:S(2)}, u32[]{:S(2)}) async-start(bf16[4,2,384]{2,1,0:T(2,128)(2,1)} %reshape.555), calls=%async_computation.2 | async-start | bytes 12288 | tf_op jit(solution)/shard_map/all_to_all | solution.py:133
  50.6 10.2 %all-to-all-start.3 = ((bf16[4,2,16384]{2,1,0:T(2,128)(2,1)}), bf16[4,2,16384]{2,1,0:T(2,128)(2,1)S(1)}, u32[]{:S(2)}, u32[]{:S(2)}) async-start(bf16[4,2,16384]{2,1,0:T(2,128)(2,1)} %reshape.559), calls=%async_computation.3 | async-start | bytes 524288 | tf_op jit(solution)/shard_map/all_to_all | solution.py:132
  56.6 0.7 copy-start.12
  134.1 14.1 %all-to-all-start.4 = ((f32[8,32,256]{2,1,0:T(8,128)}), f32[8,32,256]{2,1,0:T(8,128)S(1)}, u32[]{:S(2)}, u32[]{:S(2)}) async-start(f32[8,32,256]{2,1,0:T(8,128)} %bitcast.44), calls=%async_computation.4 | async-start | bytes 524288 | tf_op jit(solution)/shard_map/all_to_all | solution.py:191
